TPU v7x, 256 devices: a whole 4x4x8 slice. The times are simulated.
256 devices in a mesh: elec: 4 (over z_hi, core), row: 16 (over z_lo, y), col: 4 (over x).
Axes of the slice: x: 4, y: 4, z: 8 (z_hi: 2, z_lo: 4; z = z_hi * 4 + z_lo), core: 2. Of those that a mesh axis runs over, the one named last changes fastest.
Arguments:
- fields: bfloat16 [256, 2, 512, 256], P(('elec', 'row', 'col')), may hold values from -6 to 6
- mirror_phase: float32 [512, 256], replicated, may hold values from -3.140625 to 3.140625
- tile_list: int32 [16, 4, 9, 2], P('row', 'col'), may hold values from -1 to 31, as said below
Outputs:
- csd_tiles: float32 [16, 4, 9, 2, 768, 768], P('row', 'col', None, None, 'elec')
Inputs may be any that keep to these rules, and one draw needn't show every extreme that they name: `tile_list`: each slot of row index r and col index c holds a tile (i, j) of the lower triangle, j <= i, with i equal to r or 31 - r and j congruent to c modulo the number of col indices; every such tile appears in exactly one slot of its r and c, in drawn order; the other slots hold -1 in both entries.
All inputs are finite; a program needn't handle non-finite values.
Results may differ from a plain program's by a relative error of at most 0.012.
Values may be sent and summed in bfloat16 or wider, within the bound.
No kernel may reach another device: no remote copies, remote signals or barrier semaphores. Data moves between devices by JAX's collectives and lax.ppermute only.
A program may use at most 192 MiB of HBM per device.

v0:
```python
import math
import jax
import jax.numpy as jnp
from jax import lax
from jax.sharding import PartitionSpec as P

TILE = 768


def laid_out(pieces, dim):
    shape = list(pieces.shape[1:])
    shape[dim] *= pieces.shape[0]
    return jnp.moveaxis(pieces, 0, dim).reshape(shape)


def copy_for_each(x, axis):
    length = lax.axis_size(axis)
    return lax.all_to_all(jnp.broadcast_to(x[None], (length, *x.shape)), axis, 0, 0, tiled=True)


def gathered_copies(x, axis, dim):
    return laid_out(copy_for_each(x, axis), dim)


def dft_parts(length, sign_value):
    positions = jnp.arange(length, dtype=jnp.int32)
    product = positions[:, None] * positions[None, :] % length
    angles = 2.0 * math.pi / length * product.astype(jnp.float32)
    factor = 1.0 / math.sqrt(length)
    return (jnp.cos(angles) * factor, sign_value * jnp.sin(angles) * factor)


def left_table(length, sign_value, row_limit):
    real_part, imag_part = dft_parts(length, sign_value)
    real_part = real_part[:row_limit]
    imag_part = imag_part[:row_limit]
    return jnp.stack(
        [jnp.stack([real_part, -imag_part]), jnp.stack([imag_part, real_part])]
    ).astype(jnp.bfloat16)


def right_table(length, sign_value):
    real_part, imag_part = dft_parts(length, sign_value)
    return jnp.stack(
        [jnp.stack([real_part, imag_part]), jnp.stack([-imag_part, real_part])]
    ).astype(jnp.bfloat16)


def contract(formula, left_side, right_side):
    return jnp.einsum(formula, left_side, right_side, preferred_element_type=jnp.float32)


def propagate(fields, mirror_phase, slab_rows):
    length_x = fields.shape[2]
    length_y = fields.shape[3]
    cos_phase = jnp.cos(mirror_phase)
    sin_phase = jnp.sin(mirror_phase)
    first_pass = contract("dcwx,ecxy->edwy", left_table(length_x, -1.0, length_x), fields).astype(
        jnp.bfloat16
    )
    turned = contract("ecxy,cdyz->edxz", first_pass, right_table(length_y, -1.0))
    spectrum = jnp.stack(
        [
            turned[:, 0] * cos_phase - turned[:, 1] * sin_phase,
            turned[:, 0] * sin_phase + turned[:, 1] * cos_phase,
        ],
        axis=1,
    ).astype(jnp.bfloat16)
    back_rows = contract("dcwx,ecxy->edwy", left_table(length_x, 1.0, slab_rows), spectrum).astype(
        jnp.bfloat16
    )
    slab_part = contract("ecxy,cdyz->edxz", back_rows, right_table(length_y, 1.0)).astype(
        jnp.bfloat16
    )
    return slab_part.reshape(fields.shape[0], 2, slab_rows * length_y)


def accumulate(totals, row_part, col_part, row_labels, col_labels):
    row_real = row_part[..., 0, :, :]
    row_imag = row_part[..., 1, :, :]
    col_real = col_part[..., 0, :, :]
    col_imag = col_part[..., 1, :, :]
    formula = row_labels + "sp," + col_labels + "mq->smqp"
    real_sum = contract(formula, row_real, col_real) + contract(formula, row_imag, col_imag)
    imag_sum = contract(formula, row_imag, col_real) - contract(formula, row_real, col_imag)
    return totals + jnp.stack([real_sum, imag_sum], axis=2)


def body(fields, mirror_phase, tile_list):
    electrons = fields.shape[0]
    row_devices = lax.axis_size("row")
    col_devices = lax.axis_size("col")
    elec_devices = lax.axis_size("elec")
    tile_count = 2 * row_devices
    quarter = TILE // elec_devices
    window = tile_count * TILE
    spread = tile_count // col_devices
    group_size = elec_devices * col_devices
    total_electrons = electrons * elec_devices * row_devices * col_devices
    slab_field = propagate(fields, mirror_phase, window // fields.shape[3])
    entries = tile_list[0, 0]
    tile_row = entries[:, 0]
    tile_col = entries[:, 1]
    upper_pick = (tile_row >= row_devices).astype(jnp.int32)
    column = jnp.maximum(tile_col, 0) // col_devices
    is_listed = tile_row >= 0
    zero_carry = jnp.zeros((2, spread, 2, quarter, TILE), jnp.float32)
    blocks = slab_field.reshape(electrons, 2, tile_count, TILE)
    lower_tiles = blocks[:, :, :row_devices]
    higher_tiles = jnp.flip(blocks[:, :, row_devices:], axis=2)
    row_send = jnp.transpose(jnp.stack([lower_tiles, higher_tiles], axis=3), (2, 0, 1, 3, 4))
    row_mine = lax.all_to_all(row_send, "row", split_axis=0, concat_axis=1, tiled=True)
    col_send = blocks.reshape(electrons, 2, spread, col_devices, elec_devices, quarter)
    col_send = jnp.transpose(col_send, (4, 3, 0, 1, 2, 5)).reshape(
        group_size, electrons, 2, spread * quarter
    )
    col_mine = lax.all_to_all(col_send, ("elec", "col"), split_axis=0, concat_axis=1, tiled=True)
    row_panel = lax.all_gather(row_mine, ("elec", "col"), axis=0, tiled=True)
    row_panel = row_panel.reshape(group_size, row_devices, electrons, 2, 2, TILE)
    shard_piece = gathered_copies(col_mine, "row", 0)
    piece_rows = shard_piece.shape[0]
    col_part = shard_piece.reshape(piece_rows, group_size, electrons, 2, spread, quarter)
    totals = accumulate(zero_carry, row_panel, col_part, "abe", "bae")
    flat_blocks = totals.reshape(2 * spread, 2, quarter, TILE)
    result = jnp.take(flat_blocks, upper_pick * spread + column, axis=0)
    result = jnp.where(is_listed[:, None, None, None], result, jnp.zeros_like(result))
    result = result * (1.0 / math.sqrt(total_electrons))
    return result[None, None]


def solution(mesh):
    in_specs = (P(("elec", "row", "col"), None, None, None), P(), P("row", "col", None, None))
    out_specs = P("row", "col", None, None, "elec", None)
    return jax.shard_map(body, mesh=mesh, in_specs=in_specs, out_specs=out_specs, check_vma=False)
```

profile of v0, /device:TPU:1, one launch (start us, length us, event | category | flops | bytes accessed | tf_op | source)
XLA Modules:
  0.0 209.4 jit_solution(8675355788218229331)
XLA Ops:
  6.5 0.0 copy-start
  6.5 1.0 negate_convert_fusion.1
  7.5 1.7 multiply_convert_fusion.1
  9.3 1.7 multiply_convert_fusion.3
  10.9 4.4 %negate_convert_fusion = (bf16[1,512,512]{2,1,0:T(8,128)(2,1)S(1)}, bf16[1,512,512]{2,1,0:T(8,128)(2,1)S(1)}) fusion(), kind=kLoop, calls=%fused_computation.41 | loop fusion | flops 4980736 | bytes 1048576 | tf_op jit(solution)/shard_map/convert.21
  15.3 4.0 %fusion.35 = bf16[1,512,512]{2,1,0:T(8,128)(2,1)S(1)} fusion(), kind=kLoop, calls=%fused_computation.48 | loop fusion | flops 4194304 | bytes 524288 | tf_op jit(solution)/shard_map/convert.17
  19.3 1.5 fusion.28
  20.8 2.1 copy.37
  22.9 2.8 %fusion.79 = (f32[512,256]{0,1:T(8,128)S(1)}, f32[512,256]{0,1:T(8,128)S(1)}) fusion(f32[512,256]{0,1:T(8,128)} %copy.37), kind=kLoop, calls=%fused_computation.118 | loop fusion | bytes 1572864 | tf_op jit(solution)/shard_map/sin | solution.py:57
  25.7 2.4 %fusion.72 = (bf16[1,96,512]{2,1,0:T(8,128)(2,1)}, bf16[1,96,512]{2,1,0:T(8,128)(2,1)}, bf16[1,96,512]{2,1,0:T(8,128)(2,1)}) fusion(f32[512,512]{1,0:T(8,128)} %fusion.28), kind=kLoop, calls=%fused_computation.104 | loop fusion | flops 294912 | bytes 491520 | tf_op jit(solution)/shard_map/stack | solution.py:38
  28.0 1.5 maximum_bitcast_fusion
  29.5 0.0 copy-start.5
  29.5 0.0 copy-start.6
  29.5 0.0 copy-start.7
  29.5 2.0 fusion.59
  31.6 0.0 copy-start.8
  31.6 0.0 copy-done
  31.6 0.0 copy-start.9
  31.6 3.2 %convolution_bitcast_fusion = f32[1,2,512,256]{2,3,1,0:T(8,128)S(1)} fusion(bf16[1,2,512,512]{3,2,1,0:T(8,128)(2,1)} %get-tuple-element.17, bf16[1,2,512,512]{3,2,1,0:T(8,128)(2,1)} %get-tuple-element.16, bf16[1,2,256,256]{2,3,0,1:T(8,128)(2,1)} %get-tuple-element.19, bf16[1,2,256,256]{2,3,0,1:T(8,128)(2,1)} %get-tuple-element.18, ...), kind=kOutput, calls=%fused_computation.20 | convolution fusion | flops 806879232 | bytes 4194304 | tf_op jit(solution)/shard_map/ecxy,cdyz->edxz/dot_general | solution.py:50
  34.8 0.3 fusion.63
  35.0 0.0 copy-done.5
  35.0 0.0 copy-done.6
  35.1 0.0 copy-done.7
  35.1 0.0 copy-done.8
  35.1 1.7 fusion.22
  36.8 0.1 reshape_reshape_reshape.3
  37.0 0.1 reshape.301
  37.2 0.7 copy.42
  37.9 12.4 %all-to-all-start = ((bf16[16,1,2,1536]{3,2,1,0:T(2,128)(2,1)}), bf16[16,1,2,1536]{3,2,1,0:T(2,128)(2,1)S(1)}, u32[]{:S(2)}, u32[]{:S(2)}) async-start(bf16[16,1,2,1536]{3,2,1,0:T(2,128)(2,1)} %copy.42), calls=%async_computation | async-start | bytes 196608 | tf_op jit(solution)/shard_map/all_to_all | solution.py:117
  50.3 0.1 reshape_reshape.7
  50.5 0.8 maximum_bitcast_fusion.7
  51.3 8.8 %all-to-all-done = bf16[16,1,2,1536]{3,2,1,0:T(2,128)(2,1)S(1)} async-done(((bf16[16,1,2,1536]{3,2,1,0:T(2,128)(2,1)}), bf16[16,1,2,1536]{3,2,1,0:T(2,128)(2,1)S(1)}, u32[]{:S(2)}, u32[]{:S(2)}) %all-to-all-start) | async-done | bytes 98336 | tf_op jit(solution)/shard_map/all_to_all | solution.py:117
  60.1 6.0 %all-to-all-start.2 = ((bf16[16,1,2,2,768]{4,2,3,1,0:T(2,128)(2,1)}), bf16[16,1,2,2,768]{4,2,3,1,0:T(2,128)(2,1)S(1)}, u32[]{:S(2)}, u32[]{:S(2)}) async-start(bf16[16,1,2,2,768]{4,2,3,1,0:T(2,128)(2,1)} %maximum_bitcast_fusion.7), calls=%async_computation.2 | async-start | bytes 196608 | tf_op jit(solution)/shard_map/all_to_all | solution.py:112
  66.2 7.5 %all-to-all-done.2 = bf16[16,1,2,2,768]{4,2,3,1,0:T(2,128)(2,1)S(1)} async-done(((bf16[16,1,2,2,768]{4,2,3,1,0:T(2,128)(2,1)}), bf16[16,1,2,2,768]{4,2,3,1,0:T(2,128)(2,1)S(1)}, u32[]{:S(2)}, u32[]{:S(2)}) %all-to-all-start.2) | async-done | bytes 98336 | tf_op jit(solution)/shard_map/all_to_all | solution.py:112
  73.7 1.3 broadcast_in_dim.24
  75.0 4.4 %all-to-all-start.1 = ((bf16[16,1,16,2,1536]{4,2,3,1,0:T(8,128)(2,1)}), bf16[16,1,16,2,1536]{4,2,3,1,0:T(8,128)(2,1)}, u32[]{:S(2)}, u32[]{:S(2)}) async-start(bf16[16,1,16,2,1536]{4,2,3,1,0:T(8,128)(2,1)} %broadcast_in_dim.24), calls=%async_computation.1 | async-start | bytes 3145728 | tf_op jit(solution)/shard_map/all_to_all | solution.py:18
  79.4 0.0 all-gather.3.cloned.1.call-start
  79.5 0.7 copy.47
  80.2 0.0 all-gather.3.cloned.1.call-update
  80.2 0.0 copy-done.9
  80.3 32.5 %all-to-all-done.1 = bf16[16,1,16,2,1536]{4,2,3,1,0:T(8,128)(2,1)} async-done(((bf16[16,1,16,2,1536]{4,2,3,1,0:T(8,128)(2,1)}), bf16[16,1,16,2,1536]{4,2,3,1,0:T(8,128)(2,1)}, u32[]{:S(2)}, u32[]{:S(2)}) %all-to-all-start.1) | async-done | bytes 1572896 | tf_op jit(solution)/shard_map/all_to_all | solution.py:18
  112.8 3.3 %reshape_reshape.6 = bf16[16,16,1,2,8,192]{5,4,1,3,0,2:T(8,128)(2,1)S(1)} reshape(bf16[16,1,16,2,1536]{4,2,3,1,0:T(8,128)(2,1)} %all-to-all-done.1) | data formatting | bytes 3145728 | tf_op jit(solution)/shard_map/reshape;reshape | solution.py:122
  116.1 1.5 fusion.78
  117.6 24.0 %all-gather.3.cloned.1.call-done = bf16[256,1,2,2,768]{4,3,2,1,0:T(2,128)(2,1)} async-done(((bf16[16,1,2,2,768]{4,3,2,1,0:T(2,128)(2,1)}), bf16[256,1,2,2,768]{4,3,2,1,0:T(2,128)(2,1)}) %all-gather.3.cloned.1.call-update) | async-done | bytes 1572880 | tf_op jit(solution)/shard_map/all_gather | solution.py:118
  141.6 1.6 copy.48
  143.2 0.0 copy-start.2
  143.2 0.0 copy-start.4
  143.2 4.3 %fusion.37 = f32[8,192,2,768,1]{3,1,4,2,0:T(8,128)S(1)} fusion(bf16[16,16,1,1,8,192]{5,4,1,3,0,2:T(8,128)(2,1)} %get-tuple-element.8, bf16[16,16,1,2,2,768]{5,1,0,4,3,2:T(8,128)(2,1)S(1)} %bitcast.195), kind=kOutput, calls=%fused_computation.50 | convolution fusion | flops 1207959552 | bytes 11010048 | tf_op jit(solution)/shard_map/abesp,baemq->smqp/dot_general | solution.py:50
  147.5 0.0 copy-done.4
  147.6 0.0 copy-start.3
  147.6 6.3 %fusion.36 = f32[8,192,2,768,1]{3,1,4,2,0:T(8,128)} fusion(bf16[16,16,1,1,8,192]{5,4,1,3,0,2:T(8,128)(2,1)S(1)} %copy-done.4, bf16[16,16,1,2,2,768]{5,1,0,4,3,2:T(8,128)(2,1)S(1)} %bitcast.196), kind=kOutput, calls=%fused_computation.49 | convolution fusion | flops 1207959552 | bytes 11272192 | tf_op jit(solution)/shard_map/abesp,baemq->smqp/dot_general | solution.py:50
  153.9 0.0 copy-done.2
  153.9 0.0 copy-done.3
  153.9 2.7 %fusion.3 = f32[2,8,192,768]{3,2,0,1:T(8,128)S(1)} fusion(f32[8,192,2,768,1]{3,1,4,2,0:T(8,128)S(1)} %fusion.37, bf16[16,16,1,1,8,192]{5,4,1,3,0,2:T(8,128)(2,1)S(1)} %copy-done.3, bf16[16,16,1,2,2,768]{5,1,0,4,3,2:T(8,128)(2,1)S(1)} %bitcast.197), kind=kOutput, calls=%fused_computation.8 | convolution fusion | flops 1210318848 | bytes 20709376 | tf_op jit(solution)/shard_map/abesp,baemq->smqp/dot_general | solution.py:50
  156.6 0.8 copy.50
  157.4 10.6 %fusion.2 = f32[2,8,192,768]{3,2,0,1:T(8,128)} fusion(f32[8,192,2,768,1]{3,1,4,2,0:T(8,128)} %fusion.36, bf16[16,16,1,1,8,192]{5,4,1,3,0,2:T(8,128)(2,1)} %get-tuple-element.7, bf16[16,16,1,2,2,768]{5,1,0,4,3,2:T(8,128)(2,1)} %bitcast.198), kind=kOutput, calls=%fused_computation.6 | convolution fusion | flops 1210318848 | bytes 20709376 | tf_op jit(solution)/shard_map/abesp,baemq->smqp/dot_general | solution.py:50
  168.0 4.6 %copy.51 = f32[2,8,192,768]{3,2,1,0:T(8,128)S(1)} copy(f32[2,8,192,768]{3,2,0,1:T(8,128)} %fusion.2) | data formatting | bytes 18874368 | tf_op jit(solution)/shard_map/sub | solution.py:85
  172.6 7.1 %pad_maximum_fusion = f32[16,2,192,768]{3,2,0,1:T(8,128)} fusion(f32[16,1,192,768]{3,2,0,1:T(8,128)S(1)} %bitcast.194, f32[16,1,192,768]{3,2,0,1:T(8,128)S(1)} %bitcast.193), kind=kLoop, calls=%fused_computation.1 | loop fusion | flops 4718592 | bytes 37748736 | tf_op jit(solution)/shard_map/stack | solution.py:86
  179.7 13.0 %gather_fusion = f32[9,2,192,768]{3,2,1,0:T(8,128)} fusion(f32[16,2,192,768]{3,2,0,1:T(8,128)} %pad_maximum_fusion, s32[1024]{0:T(1024)S(1)} %pad_clamp_fusion), kind=kCustom, calls=%fused_computation | custom fusion | bytes 21233700 | tf_op jit(solution)/shard_map/jit(_take)/gather | solution.py:125
  192.8 0.0 copy-start.1
  192.8 9.8 %fusion.1 = f32[1,1,9,2,192,768]{5,4,3,2,1,0:T(8,128)} fusion(f32[9,2,192,768]{3,2,1,0:T(8,128)} %gather_fusion, pred[9]{0:T(512)(128)(4,1)S(1)} %get-tuple-element.5, pred[9]{0:T(512)(128)(4,1)S(1)} %get-tuple-element.26), kind=kLoop, calls=%fused_computation.4 | loop fusion | flops 7962624 | bytes 21233682 | tf_op jit(solution)/shard_map/mul | solution.py:127
  202.5 0.0 copy-done.1
  (9 shorter events, 0.2 us)
Async XLA Ops:
  6.5 25.1 %copy-start = (bf16[1,2,512,256]{3,2,1,0:T(8,128)(2,1)S(1)}, bf16[1,2,512,256]{3,2,1,0:T(8,128)(2,1)}, u32[]{:S(2)}) copy-start(bf16[1,2,512,256]{3,2,1,0:T(8,128)(2,1)} %param.3) | copy-start | bytes 1572868
  29.5 5.5 %copy-start.5 = (bf16[1,96,512]{2,1,0:T(8,128)(2,1)S(1)}, bf16[1,96,512]{2,1,0:T(8,128)(2,1)}, u32[]{:S(2)}) copy-start(bf16[1,96,512]{2,1,0:T(8,128)(2,1)} %get-tuple-element.11) | copy-start | bytes 294916
  29.5 5.5 %copy-start.6 = (bf16[1,96,512]{2,1,0:T(8,128)(2,1)S(1)}, bf16[1,96,512]{2,1,0:T(8,128)(2,1)}, u32[]{:S(2)}) copy-start(bf16[1,96,512]{2,1,0:T(8,128)(2,1)} %get-tuple-element.12) | copy-start | bytes 294916
  29.5 5.5 %copy-start.7 = (bf16[1,96,512]{2,1,0:T(8,128)(2,1)S(1)}, bf16[1,96,512]{2,1,0:T(8,128)(2,1)}, u32[]{:S(2)}) copy-start(bf16[1,96,512]{2,1,0:T(8,128)(2,1)} %get-tuple-element.13) | copy-start | bytes 294916
  31.6 3.5 %copy-start.8 = (bf16[1,2,256,256]{2,3,1,0:T(8,128)(2,1)S(1)}, bf16[1,2,256,256]{2,3,1,0:T(8,128)(2,1)}, u32[]{:S(2)}) copy-start(bf16[1,2,256,256]{2,3,1,0:T(8,128)(2,1)} %get-tuple-element.20) | copy-start | bytes 786436
  31.6 48.6 %copy-start.9 = (s32[1,1,9,2]{2,3,1,0:T(2,128)S(1)}, s32[1,1,9,2]{2,3,1,0:T(2,128)}, u32[]{:S(2)}) copy-start(s32[1,1,9,2]{2,3,1,0:T(2,128)} %param.5) | copy-start | bytes 220
  37.9 22.2 %all-to-all-start = ((bf16[16,1,2,1536]{3,2,1,0:T(2,128)(2,1)}), bf16[16,1,2,1536]{3,2,1,0:T(2,128)(2,1)S(1)}, u32[]{:S(2)}, u32[]{:S(2)}) async-start(bf16[16,1,2,1536]{3,2,1,0:T(2,128)(2,1)} %copy.42), calls=%async_computation | async-start | bytes 196608 | tf_op jit(solution)/shard_map/all_to_all | solution.py:117
  60.1 13.5 %all-to-all-start.2 = ((bf16[16,1,2,2,768]{4,2,3,1,0:T(2,128)(2,1)}), bf16[16,1,2,2,768]{4,2,3,1,0:T(2,128)(2,1)S(1)}, u32[]{:S(2)}, u32[]{:S(2)}) async-start(bf16[16,1,2,2,768]{4,2,3,1,0:T(2,128)(2,1)} %maximum_bitcast_fusion.7), calls=%async_computation.2 | async-start | bytes 196608 | tf_op jit(solution)/shard_map/all_to_all | solution.py:112
  75.0 37.8 %all-to-all-start.1 = ((bf16[16,1,16,2,1536]{4,2,3,1,0:T(8,128)(2,1)}), bf16[16,1,16,2,1536]{4,2,3,1,0:T(8,128)(2,1)}, u32[]{:S(2)}, u32[]{:S(2)}) async-start(bf16[16,1,16,2,1536]{4,2,3,1,0:T(8,128)(2,1)} %broadcast_in_dim.24), calls=%async_computation.1 | async-start | bytes 3145728 | tf_op jit(solution)/shard_map/all_to_all | solution.py:18
  79.4 62.2 %all-gather.3.cloned.1.call-start = ((), (), s32[]{:S(2)}) async-start(), calls=%async_computation.3 | async-start | bytes 1671168 | tf_op jit(solution)/shard_map/all_gather | solution.py:118
  143.2 10.7 %copy-start.2 = (bf16[256,1,2,2,768]{4,0,3,2,1:T(8,128)(2,1)}, bf16[256,1,2,2,768]{4,0,3,2,1:T(8,128)(2,1)S(1)}, u32[]{:S(2)}) copy-start(bf16[256,1,2,2,768]{4,0,3,2,1:T(8,128)(2,1)S(1)} %copy.48) | copy-start | bytes 4718596
  143.2 4.3 %copy-start.4 = (bf16[16,16,1,1,8,192]{5,4,1,3,0,2:T(8,128)(2,1)S(1)}, bf16[16,16,1,1,8,192]{5,4,1,3,0,2:T(8,128)(2,1)}, u32[]{:S(2)}) copy-start(bf16[16,16,1,1,8,192]{5,4,1,3,0,2:T(8,128)(2,1)} %get-tuple-element.8) | copy-start | bytes 2359300
  147.6 6.4 %copy-start.3 = (bf16[16,16,1,1,8,192]{5,4,1,3,0,2:T(8,128)(2,1)S(1)}, bf16[16,16,1,1,8,192]{5,4,1,3,0,2:T(8,128)(2,1)}, u32[]{:S(2)}) copy-start(bf16[16,16,1,1,8,192]{5,4,1,3,0,2:T(8,128)(2,1)} %get-tuple-element.7) | copy-start | bytes 2359300
  192.8 9.8 %copy-start.1 = (bf16[1,2,512,256]{3,2,1,0:T(8,128)(2,1)S(1)}, bf16[1,2,512,256]{3,2,1,0:T(8,128)(2,1)}, u32[]{:S(2)}) copy-start(bf16[1,2,512,256]{3,2,1,0:T(8,128)(2,1)} %param.3) | copy-start | bytes 1572868
Sparse Core Ops, SparseCore 0:
  83.0 58.5 all-gather.2
where the time goes:
time: 210 us; the launch traced here: 209 us
  waiting for transfers between devices  72.9 us (35%)
  other arithmetic  38.2 us (18%)
  local copies, waits for them, and re-layouts  33.1 us (16%)
  matrix products  28.7 us (14%)
  starting transfers between devices  22.9 us (11%)
  between operations  13.7 us (7%)
    all_to_all x1, waiting for transfers between devices, copy_for_each(): lax.all_to_all(jnp.broadcast_to(x[None], (length, *x.shape)), axis, 0, 0,...  32.5 us
    dot_general x6, matrix products, contract(): jnp.einsum(formula, left_side, right_side, preferred_element_type=jnp.flo...  28.7 us
    all_gather x1, waiting for transfers between devices, body(): row_panel = lax.all_gather(row_mine, ('elec', 'col'), axis=0, tiled=True)  24 us
    gather x1, local copies, waits for them, and re-layouts, body(): result = jnp.take(flat_blocks, upper_pick * spread + column, axis=0)  13 us
    another operation x5, other arithmetic  12.8 us
    all_to_all x1, starting transfers between devices, body(): lax.all_to_all(col_send, ('elec', 'col'), split_axis=0, concat_axis=1, ti...  12.4 us
    mul x1, other arithmetic, body(): result = result * (1.0 / math.sqrt(total_electrons))  9.79 us
    all_to_all x1, waiting for transfers between devices, body(): lax.all_to_all(col_send, ('elec', 'col'), split_axis=0, concat_axis=1, ti...  8.81 us
  transfers between devices with their start and end apart: 4, of which 4 were waited for; matrix products, arithmetic and copies ran while one was open for 3% of the time, Pallas kernels for 0%

commit v1 on v0

--- a/solution.py
+++ b/solution.py
@@ -115,7 +115,12 @@
         group_size, electrons, 2, spread * quarter
     )
     col_mine = lax.all_to_all(col_send, ("elec", "col"), split_axis=0, concat_axis=1, tiled=True)
-    row_panel = lax.all_gather(row_mine, ("elec", "col"), axis=0, tiled=True)
+    pile = []
+    for _ in range(jax.lax.axis_size(("elec", "col"))):
+        pile.append(row_mine)
+    outcome_arr = jnp.stack(pile, 0)
+    kept_arr = jax.lax.all_to_all(outcome_arr, ("elec", "col"), 0, 0)
+    row_panel = jnp.concatenate(kept_arr, 0)
     row_panel = row_panel.reshape(group_size, row_devices, electrons, 2, 2, TILE)
     shard_piece = gathered_copies(col_mine, "row", 0)
     piece_rows = shard_piece.shape[0]

time: 210 us -> 218 us (1.038)
  the two profiles are of different devices: /device:TPU:1 before, /device:TPU:32 now
where the time goes in v1:
time: 218 us
  waiting for transfers between devices  89.5 us (41%)
  other arithmetic  38.2 us (18%)
  local copies, waits for them, and re-layouts  33.8 us (16%)
  matrix products  28.7 us (13%)
  starting transfers between devices  27.2 us (12%)
    all_to_all x1, waiting for transfers between devices, body(): kept_arr = jax.lax.all_to_all(outcome_arr, ('elec', 'col'), 0, 0)  37.6 us
    all_to_all x1, waiting for transfers between devices, copy_for_each(): lax.all_to_all(jnp.broadcast_to(x[None], (length, *x.shape)), axis, 0, 0,...  36.1 us
    dot_general x6, matrix products, contract(): jnp.einsum(formula, left_side, right_side, preferred_element_type=jnp.flo...  28.7 us
    gather x1, local copies, waits for them, and re-layouts, body(): result = jnp.take(flat_blocks, upper_pick * spread + column, axis=0)  13 us
    another operation x5, other arithmetic  12.8 us
    all_to_all x1, starting transfers between devices, body(): lax.all_to_all(col_send, ('elec', 'col'), split_axis=0, concat_axis=1, ti...  10.1 us
    mul x1, other arithmetic, body(): result = result * (1.0 / math.sqrt(total_electrons))  9.79 us
    all_to_all x1, waiting for transfers between devices, body(): lax.all_to_all(col_send, ('elec', 'col'), split_axis=0, concat_axis=1, ti...  9.09 us
  transfers between devices with their start and end apart: 4, of which 4 were waited for; matrix products, arithmetic and copies ran while one was open for 3% of the time, Pallas kernels for 0%

profile of v1, /device:TPU:32, one launch (start us, length us, event | category | flops | bytes accessed | tf_op | source)
XLA Modules:
  0.0 217.6 jit_solution(13212263712704413773)
XLA Ops:
  0.0 0.0 copy-start
  0.0 1.0 negate_convert_fusion.1
  1.0 1.7 multiply_convert_fusion.1
  2.7 1.7 multiply_convert_fusion.3
  4.4 4.4 %negate_convert_fusion = (bf16[1,512,512]{2,1,0:T(8,128)(2,1)S(1)}, bf16[1,512,512]{2,1,0:T(8,128)(2,1)S(1)}) fusion(), kind=kLoop, calls=%fused_computation.42 | loop fusion | flops 4980736 | bytes 1048576 | tf_op jit(solution)/shard_map/convert.21
  8.8 4.0 %fusion.35 = bf16[1,512,512]{2,1,0:T(8,128)(2,1)S(1)} fusion(), kind=kLoop, calls=%fused_computation.49 | loop fusion | flops 4194304 | bytes 524288 | tf_op jit(solution)/shard_map/convert.17
  12.8 1.5 fusion.28
  14.3 2.1 copy.22
  16.3 2.8 %fusion.79 = (f32[512,256]{0,1:T(8,128)S(1)}, f32[512,256]{0,1:T(8,128)S(1)}) fusion(f32[512,256]{0,1:T(8,128)} %copy.22), kind=kLoop, calls=%fused_computation.119 | loop fusion | bytes 1572864 | tf_op jit(solution)/shard_map/sin | solution.py:57
  19.1 2.4 %fusion.72 = (bf16[1,96,512]{2,1,0:T(8,128)(2,1)}, bf16[1,96,512]{2,1,0:T(8,128)(2,1)}, bf16[1,96,512]{2,1,0:T(8,128)(2,1)}) fusion(f32[512,512]{1,0:T(8,128)} %fusion.28), kind=kLoop, calls=%fused_computation.105 | loop fusion | flops 294912 | bytes 491520 | tf_op jit(solution)/shard_map/stack | solution.py:38
  21.5 1.5 maximum_bitcast_fusion
  23.0 0.0 copy-start.6
  23.0 0.0 copy-start.7
  23.0 0.0 copy-start.8
  23.0 2.0 fusion.59
  25.1 0.0 copy-start.9
  25.1 0.0 copy-done
  25.1 3.2 %convolution_bitcast_fusion = f32[1,2,512,256]{2,3,1,0:T(8,128)S(1)} fusion(bf16[1,2,512,512]{3,2,1,0:T(8,128)(2,1)} %get-tuple-element.17, bf16[1,2,512,512]{3,2,1,0:T(8,128)(2,1)} %get-tuple-element.16, bf16[1,2,256,256]{2,3,0,1:T(8,128)(2,1)} %get-tuple-element.19, bf16[1,2,256,256]{2,3,0,1:T(8,128)(2,1)} %get-tuple-element.18, ...), kind=kOutput, calls=%fused_computation.21 | convolution fusion | flops 806879232 | bytes 4194304 | tf_op jit(solution)/shard_map/ecxy,cdyz->edxz/dot_general | solution.py:50
  28.2 0.0 copy-start.10
  28.2 0.3 fusion.63
  28.5 0.0 copy-done.6
  28.5 0.0 copy-done.7
  28.5 0.0 copy-done.8
  28.6 0.0 copy-done.9
  28.6 1.7 fusion.22
  30.3 0.1 reshape_reshape_reshape.3
  30.5 0.1 reshape.303
  30.6 0.7 copy.27
  31.4 10.1 %all-to-all-start = ((bf16[16,1,2,1536]{3,2,1,0:T(2,128)(2,1)}), bf16[16,1,2,1536]{3,2,1,0:T(2,128)(2,1)S(1)}, u32[]{:S(2)}, u32[]{:S(2)}) async-start(bf16[16,1,2,1536]{3,2,1,0:T(2,128)(2,1)} %copy.27), calls=%async_computation | async-start | bytes 196608 | tf_op jit(solution)/shard_map/all_to_all | solution.py:117
  41.5 0.1 reshape_reshape.10
  41.7 0.8 maximum_bitcast_fusion.7
  42.5 9.1 %all-to-all-done = bf16[16,1,2,1536]{3,2,1,0:T(2,128)(2,1)S(1)} async-done(((bf16[16,1,2,1536]{3,2,1,0:T(2,128)(2,1)}), bf16[16,1,2,1536]{3,2,1,0:T(2,128)(2,1)S(1)}, u32[]{:S(2)}, u32[]{:S(2)}) %all-to-all-start) | async-done | bytes 98336 | tf_op jit(solution)/shard_map/all_to_all | solution.py:117
  51.6 6.9 %all-to-all-start.2 = ((bf16[16,1,2,2,768]{4,2,3,1,0:T(2,128)(2,1)}), bf16[16,1,2,2,768]{4,2,3,1,0:T(2,128)(2,1)S(1)}, u32[]{:S(2)}, u32[]{:S(2)}) async-start(bf16[16,1,2,2,768]{4,2,3,1,0:T(2,128)(2,1)} %maximum_bitcast_fusion.7), calls=%async_computation.2 | async-start | bytes 196608 | tf_op jit(solution)/shard_map/all_to_all | solution.py:112
  58.6 6.7 %all-to-all-done.2 = bf16[16,1,2,2,768]{4,2,3,1,0:T(2,128)(2,1)S(1)} async-done(((bf16[16,1,2,2,768]{4,2,3,1,0:T(2,128)(2,1)}), bf16[16,1,2,2,768]{4,2,3,1,0:T(2,128)(2,1)S(1)}, u32[]{:S(2)}, u32[]{:S(2)}) %all-to-all-start.2) | async-done | bytes 98336 | tf_op jit(solution)/shard_map/all_to_all | solution.py:112
  65.3 1.3 broadcast_in_dim.24
  66.6 5.5 %all-to-all-start.1 = ((bf16[16,1,16,2,1536]{4,2,3,1,0:T(8,128)(2,1)}), bf16[16,1,16,2,1536]{4,2,3,1,0:T(8,128)(2,1)S(1)}, u32[]{:S(2)}, u32[]{:S(2)}) async-start(bf16[16,1,16,2,1536]{4,2,3,1,0:T(8,128)(2,1)} %broadcast_in_dim.24), calls=%async_computation.1 | async-start | bytes 3145728 | tf_op jit(solution)/shard_map/all_to_all | solution.py:18
  72.2 36.1 %all-to-all-done.1 = bf16[16,1,16,2,1536]{4,2,3,1,0:T(8,128)(2,1)S(1)} async-done(((bf16[16,1,16,2,1536]{4,2,3,1,0:T(8,128)(2,1)}), bf16[16,1,16,2,1536]{4,2,3,1,0:T(8,128)(2,1)S(1)}, u32[]{:S(2)}, u32[]{:S(2)}) %all-to-all-start.1) | async-done | bytes 1572896 | tf_op jit(solution)/shard_map/all_to_all | solution.py:18
  108.3 0.0 copy-start.2
  108.3 1.5 stack.184
  109.7 4.6 %all-to-all-start.3 = ((bf16[16,1,16,2,2,768]{5,2,4,3,1,0:T(8,128)(2,1)}), bf16[16,1,16,2,2,768]{5,2,4,3,1,0:T(8,128)(2,1)}, u32[]{:S(2)}, u32[]{:S(2)}) async-start(bf16[16,1,16,2,2,768]{5,2,4,3,1,0:T(8,128)(2,1)} %stack.184), calls=%async_computation.3 | async-start | bytes 3145728 | tf_op jit(solution)/shard_map/all_to_all | solution.py:122
  114.3 0.0 copy-done.10
  114.4 0.0 copy-done.2
  114.4 3.3 %reshape_reshape.9 = bf16[16,16,1,2,8,192]{5,4,1,3,0,2:T(8,128)(2,1)S(1)} reshape(bf16[16,1,16,2,1536]{4,2,3,1,0:T(8,128)(2,1)} %copy-done.2) | data formatting | bytes 3145728 | tf_op jit(solution)/shard_map/reshape;reshape | solution.py:127
  117.7 1.5 fusion.78
  119.2 37.6 %all-to-all-done.3 = bf16[16,1,16,2,2,768]{5,2,4,3,1,0:T(8,128)(2,1)} async-done(((bf16[16,1,16,2,2,768]{5,2,4,3,1,0:T(8,128)(2,1)}), bf16[16,1,16,2,2,768]{5,2,4,3,1,0:T(8,128)(2,1)}, u32[]{:S(2)}, u32[]{:S(2)}) %all-to-all-start.3) | async-done | bytes 1572896 | tf_op jit(solution)/shard_map/all_to_all | solution.py:122
  156.8 1.5 copy.63
  158.3 0.0 copy-start.3
  158.3 0.0 copy-start.5
  158.3 4.3 %fusion.37 = f32[8,192,2,768,1]{3,1,4,2,0:T(8,128)S(1)} fusion(bf16[16,16,1,1,8,192]{5,4,1,3,0,2:T(8,128)(2,1)} %get-tuple-element.8, bf16[16,16,1,2,2,768]{5,1,0,4,3,2:T(8,128)(2,1)S(1)} %bitcast.198), kind=kOutput, calls=%fused_computation.51 | convolution fusion | flops 1207959552 | bytes 11010048 | tf_op jit(solution)/shard_map/abesp,baemq->smqp/dot_general | solution.py:50
  162.6 0.0 copy-done.5
  162.7 0.0 copy-start.4
  162.7 6.3 %fusion.36 = f32[8,192,2,768,1]{3,1,4,2,0:T(8,128)} fusion(bf16[16,16,1,1,8,192]{5,4,1,3,0,2:T(8,128)(2,1)S(1)} %copy-done.5, bf16[16,16,1,2,2,768]{5,1,0,4,3,2:T(8,128)(2,1)S(1)} %bitcast.199), kind=kOutput, calls=%fused_computation.50 | convolution fusion | flops 1207959552 | bytes 11272192 | tf_op jit(solution)/shard_map/abesp,baemq->smqp/dot_general | solution.py:50
  169.0 0.0 copy-done.3
  169.0 0.0 copy-done.4
  169.0 2.7 %fusion.3 = f32[2,8,192,768]{3,2,0,1:T(8,128)S(1)} fusion(f32[8,192,2,768,1]{3,1,4,2,0:T(8,128)S(1)} %fusion.37, bf16[16,16,1,1,8,192]{5,4,1,3,0,2:T(8,128)(2,1)S(1)} %copy-done.4, bf16[16,16,1,2,2,768]{5,1,0,4,3,2:T(8,128)(2,1)S(1)} %bitcast.200), kind=kOutput, calls=%fused_computation.8 | convolution fusion | flops 1210318848 | bytes 20709376 | tf_op jit(solution)/shard_map/abesp,baemq->smqp/dot_general | solution.py:50
  171.7 0.8 copy.35
  172.5 10.6 %fusion.2 = f32[2,8,192,768]{3,2,0,1:T(8,128)} fusion(f32[8,192,2,768,1]{3,1,4,2,0:T(8,128)} %fusion.36, bf16[16,16,1,1,8,192]{5,4,1,3,0,2:T(8,128)(2,1)} %get-tuple-element.7, bf16[16,16,1,2,2,768]{5,1,0,4,3,2:T(8,128)(2,1)} %bitcast.201), kind=kOutput, calls=%fused_computation.6 | convolution fusion | flops 1210318848 | bytes 20709376 | tf_op jit(solution)/shard_map/abesp,baemq->smqp/dot_general | solution.py:50
  183.1 4.6 %copy.36 = f32[2,8,192,768]{3,2,1,0:T(8,128)S(1)} copy(f32[2,8,192,768]{3,2,0,1:T(8,128)} %fusion.2) | data formatting | bytes 18874368 | tf_op jit(solution)/shard_map/sub | solution.py:85
  187.7 7.1 %pad_maximum_fusion = f32[16,2,192,768]{3,2,0,1:T(8,128)} fusion(f32[16,1,192,768]{3,2,0,1:T(8,128)S(1)} %bitcast.197, f32[16,1,192,768]{3,2,0,1:T(8,128)S(1)} %bitcast.196), kind=kLoop, calls=%fused_computation.1 | loop fusion | flops 4718592 | bytes 37748736 | tf_op jit(solution)/shard_map/stack | solution.py:86
  194.8 13.0 %gather_fusion = f32[9,2,192,768]{3,2,1,0:T(8,128)} fusion(f32[16,2,192,768]{3,2,0,1:T(8,128)} %pad_maximum_fusion, s32[1024]{0:T(1024)S(1)} %pad_clamp_fusion), kind=kCustom, calls=%fused_computation | custom fusion | bytes 21233700 | tf_op jit(solution)/shard_map/jit(_take)/gather | solution.py:130
  207.9 0.0 copy-start.1
  207.9 9.8 %fusion.1 = f32[1,1,9,2,192,768]{5,4,3,2,1,0:T(8,128)} fusion(f32[9,2,192,768]{3,2,1,0:T(8,128)} %gather_fusion, pred[9]{0:T(512)(128)(4,1)S(1)} %get-tuple-element.5, pred[9]{0:T(512)(128)(4,1)S(1)} %get-tuple-element.26), kind=kLoop, calls=%fused_computation.4 | loop fusion | flops 7962624 | bytes 21233682 | tf_op jit(solution)/shard_map/mul | solution.py:132
  217.6 0.0 copy-done.1
  (10 shorter events, 0.2 us)
Async XLA Ops:
  0.0 25.1 %copy-start = (bf16[1,2,512,256]{3,2,1,0:T(8,128)(2,1)S(1)}, bf16[1,2,512,256]{3,2,1,0:T(8,128)(2,1)}, u32[]{:S(2)}) copy-start(bf16[1,2,512,256]{3,2,1,0:T(8,128)(2,1)} %param.3) | copy-start | bytes 1572868
  23.0 5.5 %copy-start.6 = (bf16[1,96,512]{2,1,0:T(8,128)(2,1)S(1)}, bf16[1,96,512]{2,1,0:T(8,128)(2,1)}, u32[]{:S(2)}) copy-start(bf16[1,96,512]{2,1,0:T(8,128)(2,1)} %get-tuple-element.11) | copy-start | bytes 294916
  23.0 5.5 %copy-start.7 = (bf16[1,96,512]{2,1,0:T(8,128)(2,1)S(1)}, bf16[1,96,512]{2,1,0:T(8,128)(2,1)}, u32[]{:S(2)}) copy-start(bf16[1,96,512]{2,1,0:T(8,128)(2,1)} %get-tuple-element.12) | copy-start | bytes 294916
  23.0 5.5 %copy-start.8 = (bf16[1,96,512]{2,1,0:T(8,128)(2,1)S(1)}, bf16[1,96,512]{2,1,0:T(8,128)(2,1)}, u32[]{:S(2)}) copy-start(bf16[1,96,512]{2,1,0:T(8,128)(2,1)} %get-tuple-element.13) | copy-start | bytes 294916
  25.1 3.5 %copy-start.9 = (bf16[1,2,256,256]{2,3,1,0:T(8,128)(2,1)S(1)}, bf16[1,2,256,256]{2,3,1,0:T(8,128)(2,1)}, u32[]{:S(2)}) copy-start(bf16[1,2,256,256]{2,3,1,0:T(8,128)(2,1)} %get-tuple-element.20) | copy-start | bytes 786436
  28.2 86.1 %copy-start.10 = (s32[1,1,9,2]{2,3,1,0:T(2,128)S(1)}, s32[1,1,9,2]{2,3,1,0:T(2,128)}, u32[]{:S(2)}) copy-start(s32[1,1,9,2]{2,3,1,0:T(2,128)} %param.5) | copy-start | bytes 220
  31.4 20.2 %all-to-all-start = ((bf16[16,1,2,1536]{3,2,1,0:T(2,128)(2,1)}), bf16[16,1,2,1536]{3,2,1,0:T(2,128)(2,1)S(1)}, u32[]{:S(2)}, u32[]{:S(2)}) async-start(bf16[16,1,2,1536]{3,2,1,0:T(2,128)(2,1)} %copy.27), calls=%async_computation | async-start | bytes 196608 | tf_op jit(solution)/shard_map/all_to_all | solution.py:117
  51.6 13.7 %all-to-all-start.2 = ((bf16[16,1,2,2,768]{4,2,3,1,0:T(2,128)(2,1)}), bf16[16,1,2,2,768]{4,2,3,1,0:T(2,128)(2,1)S(1)}, u32[]{:S(2)}, u32[]{:S(2)}) async-start(bf16[16,1,2,2,768]{4,2,3,1,0:T(2,128)(2,1)} %maximum_bitcast_fusion.7), calls=%async_computation.2 | async-start | bytes 196608 | tf_op jit(solution)/shard_map/all_to_all | solution.py:112
  66.6 41.7 %all-to-all-start.1 = ((bf16[16,1,16,2,1536]{4,2,3,1,0:T(8,128)(2,1)}), bf16[16,1,16,2,1536]{4,2,3,1,0:T(8,128)(2,1)S(1)}, u32[]{:S(2)}, u32[]{:S(2)}) async-start(bf16[16,1,16,2,1536]{4,2,3,1,0:T(8,128)(2,1)} %broadcast_in_dim.24), calls=%async_computation.1 | async-start | bytes 3145728 | tf_op jit(solution)/shard_map/all_to_all | solution.py:18
  108.3 6.1 %copy-start.2 = (bf16[16,1,16,2,1536]{4,2,3,1,0:T(8,128)(2,1)}, bf16[16,1,16,2,1536]{4,2,3,1,0:T(8,128)(2,1)S(1)}, u32[]{:S(2)}) copy-start(bf16[16,1,16,2,1536]{4,2,3,1,0:T(8,128)(2,1)S(1)} %all-to-all-done.1) | copy-start | bytes 4718596
  109.7 47.0 %all-to-all-start.3 = ((bf16[16,1,16,2,2,768]{5,2,4,3,1,0:T(8,128)(2,1)}), bf16[16,1,16,2,2,768]{5,2,4,3,1,0:T(8,128)(2,1)}, u32[]{:S(2)}, u32[]{:S(2)}) async-start(bf16[16,1,16,2,2,768]{5,2,4,3,1,0:T(8,128)(2,1)} %stack.184), calls=%async_computation.3 | async-start | bytes 3145728 | tf_op jit(solution)/shard_map/all_to_all | solution.py:122
  158.3 10.7 %copy-start.3 = (bf16[16,1,16,2,2,768]{5,2,0,4,3,1:T(8,128)(2,1)}, bf16[16,1,16,2,2,768]{5,2,0,4,3,1:T(8,128)(2,1)S(1)}, u32[]{:S(2)}) copy-start(bf16[16,1,16,2,2,768]{5,2,0,4,3,1:T(8,128)(2,1)S(1)} %copy.63) | copy-start | bytes 4718596
  158.3 4.3 %copy-start.5 = (bf16[16,16,1,1,8,192]{5,4,1,3,0,2:T(8,128)(2,1)S(1)}, bf16[16,16,1,1,8,192]{5,4,1,3,0,2:T(8,128)(2,1)}, u32[]{:S(2)}) copy-start(bf16[16,16,1,1,8,192]{5,4,1,3,0,2:T(8,128)(2,1)} %get-tuple-element.8) | copy-start | bytes 2359300
  162.7 6.4 %copy-start.4 = (bf16[16,16,1,1,8,192]{5,4,1,3,0,2:T(8,128)(2,1)S(1)}, bf16[16,16,1,1,8,192]{5,4,1,3,0,2:T(8,128)(2,1)}, u32[]{:S(2)}) copy-start(bf16[16,16,1,1,8,192]{5,4,1,3,0,2:T(8,128)(2,1)} %get-tuple-element.7) | copy-start | bytes 2359300
  207.9 9.8 %copy-start.1 = (bf16[1,2,512,256]{3,2,1,0:T(8,128)(2,1)S(1)}, bf16[1,2,512,256]{3,2,1,0:T(8,128)(2,1)}, u32[]{:S(2)}) copy-start(bf16[1,2,512,256]{3,2,1,0:T(8,128)(2,1)} %param.3) | copy-start | bytes 1572868
